TPU v7x, 128 devices: a whole 4x4x4 slice. The times are simulated.
128 devices in a mesh: grp: 8 (over z, x_lo), lane: 16 (over y, x_hi, core).
Axes of the slice: x: 4 (x_hi: 2, x_lo: 2; x = x_hi * 2 + x_lo), y: 4, z: 4, core: 2. Of those that a mesh axis runs over, the one named last changes fastest.
Arguments:
- factor_left: float32 [4194304], P(('grp', 'lane')), may hold values from -7 to 7, as said below
- denom_right: float32 [4194304], P(('grp', 'lane')), may hold values from -7 to 7, as said below
- bessel_left: float32 [4194304], P(('grp', 'lane')), may hold values from -7 to 7, as said below
- bessel_right: float32 [4194304], P(('grp', 'lane')), may hold values from -7 to 7, as said below
- harmonic_left: float32 [4194304], P(('grp', 'lane')), may hold values from -7 to 7, as said below
- harmonic_right: float32 [4194304], P(('grp', 'lane')), may hold values from -7 to 7, as said below
- weighted_left: float32 [4194304], P(('grp', 'lane')), may hold values from -7 to 7, as said below
Outputs:
- bessel_sum: float32 [8388608], P(('grp', 'lane'))
- harmonic_sum: float32 [8388608], P(('grp', 'lane'))
Inputs may be any that keep to these rules, and one draw needn't show every extreme that they name: `factor_left`: every limb is a whole number. `denom_right`: every limb is a whole number. `bessel_left`: every limb is a whole number. `bessel_right`: every limb is a whole number. `harmonic_left`: every limb is a whole number. `harmonic_right`: every limb is a whole number. `weighted_left`: every limb is a whole number.
All inputs are finite; a program needn't handle non-finite values.
Results may differ from a plain program's by a relative error of at most 0.00045.
Values sent between devices are 32-bit elements; how exact they have to be, the bound alone decides.
A program may use at most 128 MiB of HBM per device.

v0:
```python
import functools
import math

import jax
import jax.numpy as jnp
import numpy as np
from jax import lax
from jax.experimental import pallas as pl
from jax.experimental.pallas import tpu as pltpu
from jax.sharding import PartitionSpec as P

AXES = ("grp", "lane")
DEVICES = 128
BLOCK = 32768
ROWS = 256
COLS = 128
OPERANDS = 7
OUTPUTS = 2
DECAY = math.exp(-1.0 / (2 * BLOCK))
FIRST = 4 * OPERANDS
SECOND = 16


def split(table):
    high = table.astype(jnp.bfloat16)
    low = (table - high.astype(np.float64)).astype(jnp.bfloat16)
    return high, low


def as_real(table):
    return np.block([[table.real, -table.imag], [table.imag, table.real]])


def unit(turns):
    return np.exp(2j * math.pi * (turns % 1.0))


@functools.lru_cache(maxsize=None)
def tables():
    row = np.arange(ROWS, dtype=np.float64)
    col = np.arange(COLS, dtype=np.float64)
    rows_forward = unit(np.outer(row, row) / ROWS + row[None, :] / (4 * ROWS))
    twist = unit(np.outer(row + 0.25, col) / BLOCK)
    cols_forward = unit(np.outer(col, col) / COLS)
    blocks = np.arange(DEVICES, dtype=np.float64)
    points = np.arange(2 * DEVICES, dtype=np.float64)
    over_blocks = unit(np.outer(points, blocks) / (2 * DEVICES))
    total = DEVICES * BLOCK
    scaling = 1.0 / (16.0 * math.sqrt(total) * math.sqrt(BLOCK)) / (2 * DEVICES) / BLOCK
    order = np.concatenate([2 * blocks, 2 * blocks + 1])
    back_blocks = (
        scaling
        * unit(-np.outer(order, points) / (2 * DEVICES))
        * (1.0 - 1j * unit(points / (2 * DEVICES)))[None, :]
    )
    cols_back = unit(-np.outer(col, col) / COLS)
    rows_back = unit(-(np.outer(row, row) / ROWS + row[:, None] / (4 * ROWS)))
    offset = col[None, :] - col[:, None]
    inside = np.where(offset >= 0, DECAY ** np.maximum(offset, 0), 0.0)
    ends = np.outer(DECAY ** (COLS - 1 - col), DECAY ** (col + 1))
    line = np.arange(2 * ROWS, dtype=np.float64)
    gap = line[:, None] - line[None, :] - 1
    across = np.where(gap >= 0, DECAY ** (COLS * np.maximum(gap, 0)), 0.0)
    forward = (
        *split(np.concatenate([rows_forward.real, rows_forward.imag])),
        twist.real.astype(np.float32),
        twist.imag.astype(np.float32),
        *split(as_real(cols_forward).T),
    )
    middle = (*split(as_real(over_blocks)), *split(as_real(back_blocks)))
    backward = (
        *split(as_real(cols_back).T),
        *split(np.concatenate([rows_back.real, -rows_back.imag], axis=1)),
        *split(np.concatenate([inside, ends], axis=1)),
        *split(across),
    )
    return forward, middle, backward


def halves(values):
    high = values.astype(jnp.bfloat16)
    low = (values - high.astype(jnp.float32)).astype(jnp.bfloat16)
    return high, low


def dot(left, right):
    return jnp.dot(left, right, preferred_element_type=jnp.float32)


def times_table(values, table):
    high, low = halves(values)
    return dot(high, table[0][...]) + dot(high, table[1][...]) + dot(low, table[0][...])


def table_times(table, values):
    high, low = halves(values)
    return dot(table[0][...], high) + dot(table[1][...], high) + dot(table[0][...], low)


def complex_times(left, right):
    return (left[0] * right[0] - left[1] * right[1], left[0] * right[1] + left[1] * right[0])


def forward_kernel(*refs):
    limbs = refs[:OPERANDS]
    rows_high, rows_low, twist_real, twist_imag, cols_high, cols_low, out = refs[OPERANDS:]
    for k in range(OPERANDS):
        whole = limbs[k][...].astype(jnp.bfloat16)
        first = dot(rows_high[...], whole) + dot(rows_low[...], whole)
        turned = complex_times(
            (first[:ROWS], first[ROWS:]), (twist_real[...], twist_imag[...])
        )
        done = times_table(jnp.concatenate(turned, axis=1), (cols_high, cols_low))
        for s in range(2):
            for c in range(2):
                out[pl.ds(4 * k + 2 * s + c, DEVICES, stride=FIRST), :] = done[
                    s * DEVICES : (s + 1) * DEVICES, c * COLS : (c + 1) * COLS
                ]


def middle_kernel(landed, over_high, over_low, back_high, back_low, out):
    def spectrum(k):
        parts = [
            jnp.concatenate(
                [
                    landed[pl.ds(4 * k + 2 * s + c, DEVICES, stride=FIRST), :]
                    for s in range(2)
                ],
                axis=1,
            )
            for c in range(2)
        ]
        both = table_times((over_high, over_low), jnp.concatenate(parts, axis=0))
        return both[: 2 * DEVICES], both[2 * DEVICES :]

    factor, denom, bessel_left, bessel_right, harmonic_left, harmonic_right, weighted = [
        spectrum(k) for k in range(OPERANDS)
    ]

    def added(pairs):
        terms = [complex_times(a, b) for a, b in pairs]
        return sum(t[0] for t in terms), sum(t[1] for t in terms)

    bessel = added([(bessel_left, denom), (factor, bessel_right)])
    harmonic = added(
        [(harmonic_left, denom), (factor, harmonic_right), (weighted, bessel_right)]
    )
    for number, product in enumerate((bessel, harmonic)):
        back = table_times((back_high, back_low), jnp.concatenate(product, axis=0))
        for c in range(2):
            for odd in range(2):
                for s in range(2):
                    start = (2 * c + odd) * DEVICES
                    out[
                        pl.ds(((2 * number + odd) * 2 + s) * 2 + c, DEVICES, stride=SECOND), :
                    ] = back[start : start + DEVICES, s * COLS : (s + 1) * COLS]


def backward_kernel(landed, twist_real, twist_imag, *refs):
    cols_high, cols_low, rows_high, rows_low, scan_high, scan_low, across_high, across_low = refs[:8]
    outs = refs[8:]
    for number in range(OUTPUTS):
        coeffs = []
        for odd in range(2):
            place = (2 * number + odd) * 4
            spectrum = jnp.concatenate(
                [
                    jnp.concatenate(
                        [
                            landed[pl.ds(place + 2 * s + c, DEVICES, stride=SECOND), :]
                            for c in range(2)
                        ],
                        axis=1,
                    )
                    for s in range(2)
                ],
                axis=0,
            )
            first = times_table(spectrum, (cols_high, cols_low))
            turned = complex_times(
                (first[:, :COLS], first[:, COLS:]), (twist_real[...], -twist_imag[...])
            )
            coeffs.append(
                table_times((rows_high, rows_low), jnp.concatenate(turned, axis=0))
            )
        both = times_table(jnp.concatenate(coeffs, axis=0), (scan_high, scan_low))
        outs[number][...] = both[:, :COLS] + table_times(
            (across_high, across_low), both[:, COLS:]
        )


def call(kernel, outs, args):
    return pl.pallas_call(
        kernel,
        out_shape=outs,
        in_specs=[pl.BlockSpec(memory_space=pltpu.VMEM)] * len(args),
        out_specs=jax.tree.map(lambda _: pl.BlockSpec(memory_space=pltpu.VMEM), outs),
        compiler_params=pltpu.CompilerParams(vmem_limit_bytes=48 << 20),
    )(*args)


def exchange(values):
    return lax.all_to_all(values, AXES, split_axis=0, concat_axis=0, tiled=True)


def local(*operands):
    forward, middle, backward = tables()
    limbs = [v.reshape(ROWS, COLS) for v in operands]
    sent = call(
        forward_kernel,
        jax.ShapeDtypeStruct((DEVICES * FIRST, COLS), jnp.float32),
        [*limbs, *forward],
    )
    landed = exchange(sent)
    sent = call(
        middle_kernel,
        jax.ShapeDtypeStruct((DEVICES * SECOND, COLS), jnp.float32),
        [landed, *middle],
    )
    landed = exchange(sent)
    sums = call(
        backward_kernel,
        [jax.ShapeDtypeStruct((2 * ROWS, COLS), jnp.float32)] * OUTPUTS,
        [landed, forward[2], forward[3], *backward],
    )
    sums = jnp.stack([s.reshape(-1) for s in sums])
    everyone = lax.all_gather(sums[:, -1], AXES)
    here = lax.axis_index(AXES)
    gap = here - 1 - lax.iota(jnp.int32, DEVICES)
    weight = jnp.where(gap >= 0, jnp.exp(-jnp.maximum(gap, 0).astype(jnp.float32)), 0.0)
    carry = jnp.sum(everyone * weight[:, None], axis=0)
    power = jnp.exp(-(lax.iota(jnp.float32, 2 * BLOCK) + 1.0) / (2 * BLOCK))
    sums = sums + carry[:, None] * power
    return sums[0], sums[1]


def solution(mesh):
    return jax.shard_map(
        local,
        mesh=mesh,
        in_specs=(P(AXES),) * OPERANDS,
        out_specs=(P(AXES),) * OUTPUTS,
        check_vma=False,
    )
```

profile of v0, /device:TPU:1, one launch (start us, length us, event | category | flops | bytes accessed | tf_op | source)
XLA Modules:
  0.0 162.2 jit_solution(8031994575924505623)
XLA Ops:
  0.6 0.0 copy-start.4
  0.6 0.9 copy-done.4
  1.5 0.9 copy-done.6
  2.4 0.9 copy-done.12
  3.4 0.9 copy-done.13
  4.3 0.9 copy-done.16
  5.3 0.9 copy-done.17
  6.2 0.9 copy-done.18
  7.1 0.9 copy-done.19
  8.0 0.9 copy-done.20
  8.9 0.9 copy-done.21
  9.8 0.9 copy-done.22
  10.7 0.9 copy-done.23
  11.6 0.9 copy-done.24
  12.5 3.8 %shard_map.248 = f32[3584,128]{1,0:T(8,128)S(1)} custom-call(f32[256,128]{1,0:T(8,128)S(1)} %bitcast.18, f32[256,128]{1,0:T(8,128)S(1)} %bitcast.19, f32[256,128]{1,0:T(8,128)S(1)} %bitcast.20, f32[256,128]{1,0:T(8,128)S(1)} %bitcast.21, f32[256,128]{1,0:T(8,128)S(1)} %bitcast.22, f32[256,128]{1,0:T(8,128)S(1)} %bitcast.23, f32[256,128]{1,0:T(8,128)S(1)} %bitcast.24, ...), custom_call_target="tpu_custom_call" | custom-call | tf_op jit(solution)/shard_map/pallas_call | solution.py:193
  16.3 1.5 all_to_all.14
  17.8 41.6 %all_to_all.22 = f32[128,28,128]{2,1,0:T(8,128)} all-to-all(f32[128,28,128]{2,1,0:T(8,128)} %all_to_all.14), channel_id=1, replica_groups=mesh['grp'=8,'lane'=16] {'grp','lane'}, dimensions={0} | all-to-all | bytes 3670016 | tf_op jit(solution)/shard_map/all_to_all | solution.py:203
  59.4 1.7 %all_to_all.16.landed = f32[3584,128]{1,0:T(8,128)S(1)} reshape(f32[128,28,128]{2,1,0:T(8,128)} %all_to_all.22) | data formatting | bytes 3670016 | tf_op jit(solution)/shard_map/all_to_all | solution.py:203
  61.2 0.0 copy-done.2
  61.2 0.1 copy-done.3
  61.2 0.1 copy-done.10
  61.3 0.1 copy-done.11
  61.4 3.9 %shard_map.249 = f32[2048,128]{1,0:T(8,128)} custom-call(f32[3584,128]{1,0:T(8,128)S(1)} %all_to_all.16.landed, bf16[512,256]{1,0:T(8,128)(2,1)S(1)} %copy-done.10, bf16[512,256]{1,0:T(8,128)(2,1)S(1)} %copy-done.11, bf16[512,512]{1,0:T(8,128)(2,1)S(1)} %copy-done.2, bf16[512,512]{1,0:T(8,128)(2,1)S(1)} %copy-done.3), custom_call_target="tpu_custom_call" | custom-call | tf_op jit(solution)/shard_map/pallas_call | solution.py:193
  65.2 0.0 copy-start.8
  65.3 0.0 copy-start.9
  65.3 0.0 copy-start.14
  65.3 4.8 %all-to-all-start.1 = ((f32[128,16,128]{2,1,0:T(8,128)}), f32[128,16,128]{2,1,0:T(8,128)S(1)}, u32[]{:S(2)}, u32[]{:S(2)}) async-start(f32[128,16,128]{2,1,0:T(8,128)} %bitcast.7), calls=%async_computation.1 | async-start | bytes 2097152 | tf_op jit(solution)/shard_map/all_to_all | solution.py:203
  70.1 0.8 multiply_exponential_fusion
  70.9 18.4 %all-to-all-done.1 = f32[128,16,128]{2,1,0:T(8,128)S(1)} async-done(((f32[128,16,128]{2,1,0:T(8,128)}), f32[128,16,128]{2,1,0:T(8,128)S(1)}, u32[]{:S(2)}, u32[]{:S(2)}) %all-to-all-start.1) | async-done | bytes 1048608 | tf_op jit(solution)/shard_map/all_to_all | solution.py:203
  89.3 0.0 copy-done
  89.3 0.0 copy-done.1
  89.3 0.0 copy-done.5
  89.3 0.0 copy-done.7
  89.3 0.0 copy-done.8
  89.3 0.0 copy-done.9
  89.3 0.0 copy-done.14
  89.3 0.0 copy-start.15
  89.4 0.9 copy-done.15
  90.3 0.8 copy-done.25
  91.1 0.8 copy-done.26
  91.9 4.3 %shard_map.250 = (f32[512,128]{1,0:T(8,128)S(1)}, f32[512,128]{1,0:T(8,128)S(1)}) custom-call(f32[2048,128]{1,0:T(8,128)S(1)} %bitcast.13, f32[256,128]{1,0:T(8,128)S(1)} %copy-done.5, f32[256,128]{1,0:T(8,128)S(1)} %copy-done.7, bf16[256,256]{1,0:T(8,128)(2,1)S(1)} %copy-done.14, bf16[256,256]{1,0:T(8,128)(2,1)S(1)} %copy-done.15, ...), custom_call_target="tpu_custom_call" | custom-call | tf_op jit(solution)/shard_map/pallas_call | solution.py:193
  96.3 0.2 fusion.2
  96.5 0.2 dynamic-update-slice
  96.7 62.6 %all-reduce = f32[256]{0:T(256)S(1)} all-reduce(f32[256]{0:T(256)S(1)} %dynamic-update-slice), channel_id=2, replica_groups=mesh['grp'=8,'lane'=16] {'grp','lane'}, use_global_device_ids=true, to_apply=%add | all-reduce | flops 256 | bytes 2048
  159.3 0.1 reshape.54
  159.4 0.1 multiply_reduce_fusion
  159.5 1.5 fusion
  161.1 1.2 fusion.3
  (24 shorter events, 0.0 us)
Async XLA Ops:
  0.6 0.9 copy-start.4
  1.5 0.9 copy-start.6
  2.4 0.9 copy-start.12
  3.4 0.9 copy-start.13
  4.3 0.9 copy-start.16
  5.3 0.9 copy-start.17
  6.2 0.9 copy-start.18
  7.1 0.9 copy-start.19
  8.0 0.9 copy-start.20
  8.9 0.9 copy-start.21
  9.8 0.9 copy-start.22
  10.7 0.9 copy-start.23
  11.6 0.9 copy-start.24
  59.4 1.8 %copy-start.2 = (bf16[512,512]{1,0:T(8,128)(2,1)S(1)}, bf16[512,512]{1,0:T(8,128)(2,1)}, u32[]{:S(2)}) copy-start(bf16[512,512]{1,0:T(8,128)(2,1)} %constant.67.clone.back_high) | copy-start | bytes 1572868
  59.4 1.8 %copy-start.3 = (bf16[512,512]{1,0:T(8,128)(2,1)S(1)}, bf16[512,512]{1,0:T(8,128)(2,1)}, u32[]{:S(2)}) copy-start(bf16[512,512]{1,0:T(8,128)(2,1)} %constant.68.clone.back_low) | copy-start | bytes 1572868
  59.4 1.9 %copy-start.10 = (bf16[512,256]{1,0:T(8,128)(2,1)S(1)}, bf16[512,256]{1,0:T(8,128)(2,1)}, u32[]{:S(2)}) copy-start(bf16[512,256]{1,0:T(8,128)(2,1)} %constant.65.clone.over_high) | copy-start | bytes 786436
  59.4 2.0 %copy-start.11 = (bf16[512,256]{1,0:T(8,128)(2,1)S(1)}, bf16[512,256]{1,0:T(8,128)(2,1)}, u32[]{:S(2)}) copy-start(bf16[512,256]{1,0:T(8,128)(2,1)} %constant.66.clone.over_low) | copy-start | bytes 786436
  65.2 24.1 %copy-start = (bf16[512,512]{1,0:T(8,128)(2,1)S(1)}, bf16[512,512]{1,0:T(8,128)(2,1)}, u32[]{:S(2)}) copy-start(bf16[512,512]{1,0:T(8,128)(2,1)} %constant.75.clone.refs_6_) | copy-start | bytes 1572868
  65.2 24.1 %copy-start.1 = (bf16[512,512]{1,0:T(8,128)(2,1)S(1)}, bf16[512,512]{1,0:T(8,128)(2,1)}, u32[]{:S(2)}) copy-start(bf16[512,512]{1,0:T(8,128)(2,1)} %constant.76.clone.refs_7_) | copy-start | bytes 1572868
  65.2 24.1 %copy-start.5 = (f32[256,128]{1,0:T(8,128)S(1)}, f32[256,128]{1,0:T(8,128)}, u32[]{:S(2)}) copy-start(f32[256,128]{1,0:T(8,128)} %constant.61.clone.refs_9_.twist_real) | copy-start | bytes 393220
  65.2 24.1 %copy-start.7 = (f32[256,128]{1,0:T(8,128)S(1)}, f32[256,128]{1,0:T(8,128)}, u32[]{:S(2)}) copy-start(f32[256,128]{1,0:T(8,128)} %constant.62.clone.refs_10_.twist_imag) | copy-start | bytes 393220
  65.2 24.1 %copy-start.8 = (bf16[256,512]{1,0:T(8,128)(2,1)S(1)}, bf16[256,512]{1,0:T(8,128)(2,1)}, u32[]{:S(2)}) copy-start(bf16[256,512]{1,0:T(8,128)(2,1)} %constant.71.clone.refs_2_) | copy-start | bytes 786436
  65.3 24.1 %copy-start.9 = (bf16[256,512]{1,0:T(8,128)(2,1)S(1)}, bf16[256,512]{1,0:T(8,128)(2,1)}, u32[]{:S(2)}) copy-start(bf16[256,512]{1,0:T(8,128)(2,1)} %constant.72.clone.refs_3_) | copy-start | bytes 786436
  65.3 24.1 %copy-start.14 = (bf16[256,256]{1,0:T(8,128)(2,1)S(1)}, bf16[256,256]{1,0:T(8,128)(2,1)}, u32[]{:S(2)}) copy-start(bf16[256,256]{1,0:T(8,128)(2,1)} %constant.69.clone.refs_0_) | copy-start | bytes 393220
  65.3 24.0 %all-to-all-start.1 = ((f32[128,16,128]{2,1,0:T(8,128)}), f32[128,16,128]{2,1,0:T(8,128)S(1)}, u32[]{:S(2)}, u32[]{:S(2)}) async-start(f32[128,16,128]{2,1,0:T(8,128)} %bitcast.7), calls=%async_computation.1 | async-start | bytes 2097152 | tf_op jit(solution)/shard_map/all_to_all | solution.py:203
  89.3 0.9 copy-start.15
  90.3 0.8 copy-start.25
  91.1 0.8 copy-start.26
where the time goes:
time: 163 us; the launch traced here: 162 us
  blocking collectives  104 us (64%)
  local copies, waits for them, and re-layouts  19.4 us (12%)
  waiting for transfers between devices  18.4 us (11%)
  Pallas kernels  12 us (7%)
  starting transfers between devices  4.81 us (3%)
  other arithmetic  2.62 us (2%)
    unnamed x1, blocking collectives  62.6 us
    all_to_all x1, blocking collectives, exchange(): return lax.all_to_all(values, AXES, split_axis=0, concat_axis=0, tiled=True)  41.6 us
    all_to_all x1, waiting for transfers between devices, exchange(): return lax.all_to_all(values, AXES, split_axis=0, concat_axis=0, tiled=True)  18.4 us
    unnamed x56, local copies, waits for them, and re-layouts  14.9 us
    pallas_call x3, Pallas kernels, call(): pl.pallas_call(kernel, out_shape=outs, in_specs=[pl.BlockSpec(memory_spac...  12 us
    all_to_all x1, starting transfers between devices, exchange(): return lax.all_to_all(values, AXES, split_axis=0, concat_axis=0, tiled=True)  4.81 us
  transfers between devices with their start and end apart: 1, of which 1 were waited for; matrix products, arithmetic and copies ran while one was open for 1% of the time, Pallas kernels for 0%

commit v1 on v0

v1 whole, which is shorter than its diff:
```python
import functools
import math

import jax
import jax.numpy as jnp
import numpy as np
from jax import lax
from jax.experimental import pallas as pl
from jax.experimental.pallas import tpu as pltpu
from jax.sharding import PartitionSpec as P

AXES = ("grp", "lane")
DEVICES = 128
BLOCK = 32768
ROWS = 256
COLS = 128
OPERANDS = 7
OUTPUTS = 2
DECAY = math.exp(-1.0 / (2 * BLOCK))
LANES = 16
STEP_IN = 32
STEP_OUT = 16
GROUPS = ((0, 3), (2, 1), (4, 5), (6,))
MESH = pl.DeviceIdType.MESH


def split(table):
    high = table.astype(jnp.bfloat16)
    low = (table - high.astype(np.float64)).astype(jnp.bfloat16)
    return high, low


def as_real(table):
    return np.block([[table.real, -table.imag], [table.imag, table.real]])


def unit(turns):
    return np.exp(2j * math.pi * (turns % 1.0))


@functools.lru_cache(maxsize=None)
def tables():
    row = np.arange(ROWS, dtype=np.float64)
    col = np.arange(COLS, dtype=np.float64)
    rows_forward = unit(np.outer(row, row) / ROWS + row[None, :] / (4 * ROWS))
    twist = unit(np.outer(row + 0.25, col) / BLOCK)
    cols_forward = unit(np.outer(col, col) / COLS)
    blocks = np.arange(DEVICES, dtype=np.float64)
    points = np.arange(2 * DEVICES, dtype=np.float64)
    over_blocks = unit(np.outer(points, blocks) / (2 * DEVICES))
    total = DEVICES * BLOCK
    scaling = 1.0 / (16.0 * math.sqrt(total) * math.sqrt(BLOCK)) / (2 * DEVICES) / BLOCK
    order = np.concatenate([2 * blocks, 2 * blocks + 1])
    back_blocks = (
        scaling
        * unit(-np.outer(order, points) / (2 * DEVICES))
        * (1.0 - 1j * unit(points / (2 * DEVICES)))[None, :]
    )
    cols_back = unit(-np.outer(col, col) / COLS)
    rows_back = unit(-(np.outer(row, row) / ROWS + row[:, None] / (4 * ROWS)))
    offset = col[None, :] - col[:, None]
    inside = np.where(offset >= 0, DECAY ** np.maximum(offset, 0), 0.0)
    ends = np.outer(DECAY ** (COLS - 1 - col), DECAY ** (col + 1))
    line = np.arange(2 * ROWS, dtype=np.float64)
    gap = line[:, None] - line[None, :] - 1
    across = np.where(gap >= 0, DECAY ** (COLS * np.maximum(gap, 0)), 0.0)
    phase = unit((np.arange(ROWS)[:, None] + ROWS * col[None, :] + 0.25) / BLOCK)
    ends_at = DECAY**BLOCK
    reach = (ends_at / DECAY + 1j / DECAY) / (1.0 - 1.0 / (DECAY * phase))
    reach = reach.reshape(2, DEVICES, COLS).transpose(1, 0, 2)
    reach = np.concatenate([reach.real, reach.imag], axis=1)
    reach = np.concatenate([reach, np.zeros_like(reach)], axis=1).astype(np.float32)
    every = np.arange(2 * DEVICES, dtype=np.float64)
    back_all = (
        scaling
        * unit(-np.outer(every, points) / (2 * DEVICES))
        * (1.0 - 1j * unit(points / (2 * DEVICES)))[None, :]
    )
    gap = 2 * blocks[:, None] - 1 - every[None, :]
    carry = np.where(gap >= 0, ends_at ** np.maximum(gap, 0), 0.0) @ back_all
    power = DECAY ** (np.arange(2 * BLOCK, dtype=np.float64) + 1).reshape(2 * ROWS, COLS)
    forward = (
        *split(np.concatenate([rows_forward.real, rows_forward.imag])),
        twist.real.astype(np.float32),
        twist.imag.astype(np.float32),
        *split(as_real(cols_forward).T),
    )
    middle = (
        *split(as_real(over_blocks)),
        *split(as_real(back_blocks)),
        *split(np.concatenate([carry.real, -carry.imag], axis=1)),
    )
    backward = (
        *split(as_real(cols_back).T),
        *split(np.concatenate([rows_back.real, -rows_back.imag], axis=1)),
        *split(np.concatenate([inside, ends], axis=1)),
        *split(across),
    )
    return (*forward, *middle, *backward, power.astype(np.float32), reach)


def halves(values):
    high = values.astype(jnp.bfloat16)
    low = (values - high.astype(jnp.float32)).astype(jnp.bfloat16)
    return high, low


def dot(left, right):
    return jnp.dot(left, right, preferred_element_type=jnp.float32)


def times_table(values, table):
    high, low = halves(values)
    return dot(high, table[0][...]) + dot(high, table[1][...]) + dot(low, table[0][...])


def table_times(table, values):
    high, low = halves(values)
    return dot(table[0][...], high) + dot(table[1][...], high) + dot(table[0][...], low)


def complex_times(left, right):
    return (left[0] * right[0] - left[1] * right[1], left[0] * right[1] + left[1] * right[0])


def block_of(ref, start):
    return ref[pl.ds(start, DEVICES, stride=STEP_IN), :]


def merge_kernel(*refs):
    limbs_in = refs[:OPERANDS]
    count = len(tables())
    tables_in = refs[OPERANDS : OPERANDS + count - 1]
    reach_in = refs[OPERANDS + count - 1]
    outs = refs[OPERANDS + count : OPERANDS + count + OUTPUTS]
    rest = refs[OPERANDS + count + OUTPUTS :]
    limbs = rest[:OPERANDS]
    held = rest[OPERANDS : OPERANDS + count - 1]
    (
        reach,
        sent,
        landed,
        sent_back,
        landed_back,
        results,
        load_sem,
        table_sem,
        out_sem,
        send_sem,
        recv_sem,
        back_send_sem,
        back_recv_sem,
    ) = rest[OPERANDS + count - 1 :]
    (
        rows_high,
        rows_low,
        twist_real,
        twist_imag,
        cols_high,
        cols_low,
        over_high,
        over_low,
        back_high,
        back_low,
        carry_high,
        carry_low,
        cols_back_high,
        cols_back_low,
        rows_back_high,
        rows_back_low,
        scan_high,
        scan_low,
        across_high,
        across_low,
        power,
    ) = held
    me = lax.axis_index("grp") * LANES + lax.axis_index("lane")

    limb_copies = [
        pltpu.make_async_copy(limbs_in[k], limbs[k], load_sem.at[k]) for k in range(OPERANDS)
    ]
    table_copies = [
        pltpu.make_async_copy(tables_in[k], held[k], table_sem.at[k]) for k in range(count - 1)
    ]
    table_copies.append(
        pltpu.make_async_copy(reach_in.at[me], reach, table_sem.at[count - 1])
    )
    loaded = set()

    def need(*numbers):
        for k in numbers:
            if k not in loaded:
                loaded.add(k)
                table_copies[k].wait()

    first_limbs = [k for group in GROUPS for k in group]
    for k in first_limbs[:2]:
        limb_copies[k].start()
    for k in range(6):
        table_copies[k].start()
    for k in first_limbs[2:]:
        limb_copies[k].start()
    for k in range(6, count):
        table_copies[k].start()

    def partner(i):
        other = jnp.bitwise_xor(me, i)
        return other, (lax.div(other, LANES), lax.rem(other, LANES))

    barrier = pltpu.get_barrier_semaphore()

    def greet(i, _):
        pl.semaphore_signal(barrier, inc=1, device_id=partner(i)[1], device_id_type=MESH)
        return 0

    lax.fori_loop(1, DEVICES, greet, 0)

    def send(source, target, step, offset, size, send_to, recv_at):
        def go(i, _):
            other, place = partner(i)
            pltpu.make_async_remote_copy(
                src_ref=source.at[pl.ds(pl.multiple_of(other * step, 8) + offset, size)],
                dst_ref=target.at[pl.ds(pl.multiple_of(me * step, 8) + offset, size)],
                send_sem=send_to,
                recv_sem=recv_at,
                device_id=place,
                device_id_type=MESH,
            ).start()
            return 0

        lax.fori_loop(1, DEVICES, go, 0)
        here = pl.ds(pl.multiple_of(me * step, 8) + offset, size)
        target[here, :] = source[here, :]

    def wait(ref, size, sem):
        whole = ref.at[pl.ds(0, (DEVICES - 1) * size)]
        pltpu.make_async_copy(whole, whole, sem).wait()

    need(0, 1, 2, 3, 4, 5)
    for number, group in enumerate(GROUPS):
        for place, k in enumerate(group):
            limb_copies[k].wait()
            whole = limbs[k][...].astype(jnp.bfloat16)
            first = dot(rows_high[...], whole) + dot(rows_low[...], whole)
            turned = complex_times(
                (first[:ROWS], first[ROWS:]), (twist_real[...], twist_imag[...])
            )
            done = times_table(jnp.concatenate(turned, axis=1), (cols_high, cols_low))
            for s in range(2):
                for c in range(2):
                    start = 8 * number + 4 * place + 2 * s + c
                    sent[pl.ds(start, DEVICES, stride=STEP_IN), :] = done[
                        s * DEVICES : (s + 1) * DEVICES, c * COLS : (c + 1) * COLS
                    ]
        if number == 0:
            pl.semaphore_wait(barrier, DEVICES - 1)
        send(
            sent, landed, STEP_IN, 8 * number, 4 * len(group),
            send_sem.at[number], recv_sem.at[number],
        )

    spectra = [None] * OPERANDS

    def arrive(number):
        group = GROUPS[number]
        wait(landed, 4 * len(group), recv_sem.at[number])
        for place, k in enumerate(group):
            parts = [
                jnp.concatenate(
                    [block_of(landed, 8 * number + 4 * place + 2 * s + c) for s in range(2)],
                    axis=1,
                )
                for c in range(2)
            ]
            both = table_times((over_high, over_low), jnp.concatenate(parts, axis=0))
            spectra[k] = (both[: 2 * DEVICES], both[2 * DEVICES :])

    def give_back(number, terms):
        terms = [complex_times(spectra[a], spectra[b]) for a, b in terms]
        product = (sum(t[0] for t in terms), sum(t[1] for t in terms))
        back = table_times((back_high, back_low), jnp.concatenate(product, axis=0))
        source = sent_back.at[number]
        for c in range(2):
            for odd in range(2):
                for s in range(2):
                    start = (2 * c + odd) * DEVICES
                    source[pl.ds((odd * 2 + s) * 2 + c, DEVICES, stride=STEP_OUT), :] = back[
                        start : start + DEVICES, s * COLS : (s + 1) * COLS
                    ]
        reached = [
            complex_times(
                (product[0][:, s * COLS : (s + 1) * COLS], product[1][:, s * COLS : (s + 1) * COLS]),
                (reach[s : s + 1, :], reach[2 + s : 3 + s, :]),
            )
            for s in range(2)
        ]
        reached = jnp.concatenate(
            [reached[0][0] + reached[1][0], reached[0][1] + reached[1][1]], axis=0
        )
        source[pl.ds(8, DEVICES, stride=STEP_OUT), :] = table_times(
            (carry_high, carry_low), reached
        )
        send(
            source, landed_back.at[number], STEP_OUT, 0, 9,
            back_send_sem.at[number], back_recv_sem.at[number],
        )

    need(6, 7)
    arrive(0)
    arrive(1)
    need(8, 9, 10, 11, count - 1)
    give_back(0, [(2, 1), (0, 3)])
    arrive(2)
    arrive(3)
    give_back(1, [(4, 1), (0, 5), (6, 3)])

    need(*range(count))
    out_copies = []
    for number in range(OUTPUTS):
        source = landed_back.at[number]
        wait(source, 9, back_recv_sem.at[number])
        coeffs = []
        for odd in range(2):
            spectrum = jnp.concatenate(
                [
                    jnp.concatenate(
                        [
                            source[
                                pl.ds(4 * odd + 2 * s + c, DEVICES, stride=STEP_OUT), :
                            ]
                            for c in range(2)
                        ],
                        axis=1,
                    )
                    for s in range(2)
                ],
                axis=0,
            )
            first = times_table(spectrum, (cols_back_high, cols_back_low))
            turned = complex_times(
                (first[:, :COLS], first[:, COLS:]), (twist_real[...], -twist_imag[...])
            )
            coeffs.append(
                table_times((rows_back_high, rows_back_low), jnp.concatenate(turned, axis=0))
            )
        incoming = jnp.sum(source[pl.ds(8, DEVICES, stride=STEP_OUT), :])
        both = times_table(jnp.concatenate(coeffs, axis=0), (scan_high, scan_low))
        results[number] = (
            both[:, :COLS]
            + table_times((across_high, across_low), both[:, COLS:])
            + incoming * power[...]
        )
        copy = pltpu.make_async_copy(results.at[number], outs[number], out_sem.at[number])
        copy.start()
        out_copies.append(copy)

    for copy in out_copies:
        copy.wait()
    for number, group in enumerate(GROUPS):
        wait(sent, 4 * len(group), send_sem.at[number])
    for number in range(OUTPUTS):
        wait(sent_back.at[number], 9, back_send_sem.at[number])


def local(*operands):
    limbs = [v.reshape(ROWS, COLS) for v in operands]
    constants = tables()
    anywhere = pl.BlockSpec(memory_space=pl.ANY)
    sums = pl.pallas_call(
        merge_kernel,
        out_shape=[jax.ShapeDtypeStruct((2 * ROWS, COLS), jnp.float32)] * OUTPUTS,
        in_specs=[anywhere] * (OPERANDS + len(constants)),
        out_specs=[anywhere] * OUTPUTS,
        scratch_shapes=[
            *[pltpu.VMEM((ROWS, COLS), jnp.float32)] * OPERANDS,
            *[pltpu.VMEM(t.shape, t.dtype) for t in constants[:-1]],
            pltpu.VMEM(constants[-1].shape[1:], jnp.float32),
            pltpu.VMEM((DEVICES * STEP_IN, COLS), jnp.float32),
            pltpu.VMEM((DEVICES * STEP_IN, COLS), jnp.float32),
            pltpu.VMEM((OUTPUTS, DEVICES * STEP_OUT, COLS), jnp.float32),
            pltpu.VMEM((OUTPUTS, DEVICES * STEP_OUT, COLS), jnp.float32),
            pltpu.VMEM((OUTPUTS, 2 * ROWS, COLS), jnp.float32),
            pltpu.SemaphoreType.DMA((OPERANDS,)),
            pltpu.SemaphoreType.DMA((len(constants),)),
            pltpu.SemaphoreType.DMA((OUTPUTS,)),
            pltpu.SemaphoreType.DMA((len(GROUPS),)),
            pltpu.SemaphoreType.DMA((len(GROUPS),)),
            pltpu.SemaphoreType.DMA((OUTPUTS,)),
            pltpu.SemaphoreType.DMA((OUTPUTS,)),
        ],
        compiler_params=pltpu.CompilerParams(
            collective_id=0, has_side_effects=True, vmem_limit_bytes=56 << 20
        ),
    )(*limbs, *constants)
    return tuple(s.reshape(-1) for s in sums)


def solution(mesh):
    return jax.shard_map(
        local,
        mesh=mesh,
        in_specs=(P(AXES),) * OPERANDS,
        out_specs=(P(AXES),) * OUTPUTS,
        check_vma=False,
    )
```

time: 163 us -> 69.1 us (0.42)
  the two profiles are of different devices: /device:TPU:1 before, /device:TPU:3 now
where the time goes in v1:
time: 69.1 us; the launch traced here: 69 us
  Pallas kernels  65.9 us (95%)
  local copies, waits for them, and re-layouts  2.44 us (4%)
    pallas_call x1, Pallas kernels, local(): pl.pallas_call(merge_kernel, out_shape=[jax.ShapeDtypeStruct((2 * ROWS, C...  65.9 us
    unnamed x4, local copies, waits for them, and re-layouts  2.44 us

profile of v1, /device:TPU:3, one launch (start us, length us, event | category | flops | bytes accessed | tf_op | source)
XLA Modules:
  0.0 69.0 jit_solution(2814348497191664564)
XLA Ops:
  0.6 65.9 %shard_map.284 = (f32[512,128]{1,0:T(8,128)}, f32[512,128]{1,0:T(8,128)}) custom-call(f32[256,128]{1,0:T(8,128)} %bitcast.11, f32[256,128]{1,0:T(8,128)} %bitcast.12, f32[256,128]{1,0:T(8,128)} %bitcast.13, f32[256,128]{1,0:T(8,128)} %bitcast.14, f32[256,128]{1,0:T(8,128)} %bitcast.15, f32[256,128]{1,0:T(8,128)} %bitcast.16, f32[256,128]{1,0:T(8,128)} %bitcast.17, ...), custom_call_target="tpu_custom_call" | custom-call | tf_op jit(solution)/shard_map/pallas_call | solution.py:369
  66.5 0.0 copy-start
  66.6 1.7 %copy.33 = f32[65536]{0:T(1024)} copy(f32[65536]{0:T(1024)} %bitcast.10) | data formatting | bytes 524288
  68.3 0.0 copy-done
  68.3 0.7 %copy.34 = f32[65536]{0:T(1024)} copy(f32[65536]{0:T(1024)S(1)} %bitcast.9) | data formatting | bytes 524288
Async XLA Ops:
  66.5 1.7 %copy-start = (f32[512,128]{1,0:T(8,128)S(1)}, f32[512,128]{1,0:T(8,128)}, u32[]{:S(2)}) copy-start(f32[512,128]{1,0:T(8,128)} %get-tuple-element.5) | copy-start | bytes 786436

commit v2 on v1

--- a/solution.py
+++ b/solution.py
@@ -18,8 +18,9 @@
 OUTPUTS = 2
 DECAY = math.exp(-1.0 / (2 * BLOCK))
 LANES = 16
+TEAMS = 8
 STEP_IN = 32
-STEP_OUT = 16
+STEP_OUT = 8
 GROUPS = ((0, 3), (2, 1), (4, 5), (6,))
 MESH = pl.DeviceIdType.MESH
 
@@ -76,9 +77,9 @@
         * unit(-np.outer(every, points) / (2 * DEVICES))
         * (1.0 - 1j * unit(points / (2 * DEVICES)))[None, :]
     )
-    gap = 2 * blocks[:, None] - 1 - every[None, :]
+    owner = (blocks.reshape(TEAMS, LANES).T).reshape(-1)
+    gap = 2 * owner[:, None] - 1 - every[None, :]
     carry = np.where(gap >= 0, ends_at ** np.maximum(gap, 0), 0.0) @ back_all
-    power = DECAY ** (np.arange(2 * BLOCK, dtype=np.float64) + 1).reshape(2 * ROWS, COLS)
     forward = (
         *split(np.concatenate([rows_forward.real, rows_forward.imag])),
         twist.real.astype(np.float32),
@@ -96,7 +97,7 @@
         *split(np.concatenate([inside, ends], axis=1)),
         *split(across),
     )
-    return (*forward, *middle, *backward, power.astype(np.float32), reach)
+    return (*forward, *middle, *backward, reach)
 
 
 def halves(values):
@@ -132,8 +133,8 @@
     count = len(tables())
     tables_in = refs[OPERANDS : OPERANDS + count - 1]
     reach_in = refs[OPERANDS + count - 1]
-    outs = refs[OPERANDS + count : OPERANDS + count + OUTPUTS]
-    rest = refs[OPERANDS + count + OUTPUTS :]
+    sums_out, carry_out = refs[OPERANDS + count : OPERANDS + count + 2]
+    rest = refs[OPERANDS + count + 2 :]
     limbs = rest[:OPERANDS]
     held = rest[OPERANDS : OPERANDS + count - 1]
     (
@@ -143,6 +144,11 @@
         sent_back,
         landed_back,
         results,
+        owed,
+        owed_in,
+        part,
+        part_in,
+        carried,
         load_sem,
         table_sem,
         out_sem,
@@ -150,6 +156,10 @@
         recv_sem,
         back_send_sem,
         back_recv_sem,
+        owed_send_sem,
+        owed_recv_sem,
+        part_send_sem,
+        part_recv_sem,
     ) = rest[OPERANDS + count - 1 :]
     (
         rows_high,
@@ -172,9 +182,9 @@
         scan_low,
         across_high,
         across_low,
-        power,
     ) = held
-    me = lax.axis_index("grp") * LANES + lax.axis_index("lane")
+    team, lane = lax.axis_index("grp"), lax.axis_index("lane")
+    me = team * LANES + lane
 
     limb_copies = [
         pltpu.make_async_copy(limbs_in[k], limbs[k], load_sem.at[k]) for k in range(OPERANDS)
@@ -232,8 +242,8 @@
         here = pl.ds(pl.multiple_of(me * step, 8) + offset, size)
         target[here, :] = source[here, :]
 
-    def wait(ref, size, sem):
-        whole = ref.at[pl.ds(0, (DEVICES - 1) * size)]
+    def wait(ref, size, sem, senders=DEVICES):
+        whole = ref.at[pl.ds(0, (senders - 1) * size)]
         pltpu.make_async_copy(whole, whole, sem).wait()
 
     need(0, 1, 2, 3, 4, 5)
@@ -275,18 +285,12 @@
             both = table_times((over_high, over_low), jnp.concatenate(parts, axis=0))
             spectra[k] = (both[: 2 * DEVICES], both[2 * DEVICES :])
 
+    def tile(number):
+        return pl.ds(pl.multiple_of(number * 8, 8), 8)
+
     def give_back(number, terms):
         terms = [complex_times(spectra[a], spectra[b]) for a, b in terms]
         product = (sum(t[0] for t in terms), sum(t[1] for t in terms))
-        back = table_times((back_high, back_low), jnp.concatenate(product, axis=0))
-        source = sent_back.at[number]
-        for c in range(2):
-            for odd in range(2):
-                for s in range(2):
-                    start = (2 * c + odd) * DEVICES
-                    source[pl.ds((odd * 2 + s) * 2 + c, DEVICES, stride=STEP_OUT), :] = back[
-                        start : start + DEVICES, s * COLS : (s + 1) * COLS
-                    ]
         reached = [
             complex_times(
                 (product[0][:, s * COLS : (s + 1) * COLS], product[1][:, s * COLS : (s + 1) * COLS]),
@@ -297,13 +301,53 @@
         reached = jnp.concatenate(
             [reached[0][0] + reached[1][0], reached[0][1] + reached[1][1]], axis=0
         )
-        source[pl.ds(8, DEVICES, stride=STEP_OUT), :] = table_times(
-            (carry_high, carry_low), reached
-        )
+        owed[number] = table_times((carry_high, carry_low), reached)
+
+        def owe(i, _):
+            other = jnp.bitwise_xor(lane, i)
+            pltpu.make_async_remote_copy(
+                src_ref=owed.at[number, tile(other)],
+                dst_ref=owed_in.at[number, tile(lane)],
+                send_sem=owed_send_sem.at[number],
+                recv_sem=owed_recv_sem.at[number],
+                device_id=(team, other),
+                device_id_type=MESH,
+            ).start()
+            return 0
+
+        lax.fori_loop(1, LANES, owe, 0)
+        owed_in[number, tile(lane), :] = owed[number, tile(lane), :]
+        back = table_times((back_high, back_low), jnp.concatenate(product, axis=0))
+        source = sent_back.at[number]
+        for c in range(2):
+            for odd in range(2):
+                for s in range(2):
+                    start = (2 * c + odd) * DEVICES
+                    source[pl.ds((odd * 2 + s) * 2 + c, DEVICES, stride=STEP_OUT), :] = back[
+                        start : start + DEVICES, s * COLS : (s + 1) * COLS
+                    ]
         send(
-            source, landed_back.at[number], STEP_OUT, 0, 9,
+            source, landed_back.at[number], STEP_OUT, 0, 8,
             back_send_sem.at[number], back_recv_sem.at[number],
         )
+
+    def gather_owed(number):
+        wait(owed_in.at[number], 8, owed_recv_sem.at[number], LANES)
+        part[number] = sum(owed_in[number, 8 * k : 8 * k + 8, :] for k in range(LANES))
+
+        def pay(i, _):
+            pltpu.make_async_remote_copy(
+                src_ref=part.at[number],
+                dst_ref=part_in.at[number, tile(team)],
+                send_sem=part_send_sem.at[number],
+                recv_sem=part_recv_sem.at[number],
+                device_id=(jnp.bitwise_xor(team, i), lane),
+                device_id_type=MESH,
+            ).start()
+            return 0
+
+        lax.fori_loop(1, TEAMS, pay, 0)
+        part_in[number, tile(team), :] = part[number]
 
     need(6, 7)
     arrive(0)
@@ -314,11 +358,14 @@
     arrive(3)
     give_back(1, [(4, 1), (0, 5), (6, 3)])
 
+    gather_owed(0)
+    gather_owed(1)
+
     need(*range(count))
     out_copies = []
     for number in range(OUTPUTS):
         source = landed_back.at[number]
-        wait(source, 9, back_recv_sem.at[number])
+        wait(source, 8, back_recv_sem.at[number])
         coeffs = []
         for odd in range(2):
             spectrum = jnp.concatenate(
@@ -343,34 +390,74 @@
             coeffs.append(
                 table_times((rows_back_high, rows_back_low), jnp.concatenate(turned, axis=0))
             )
-        incoming = jnp.sum(source[pl.ds(8, DEVICES, stride=STEP_OUT), :])
         both = times_table(jnp.concatenate(coeffs, axis=0), (scan_high, scan_low))
-        results[number] = (
-            both[:, :COLS]
-            + table_times((across_high, across_low), both[:, COLS:])
-            + incoming * power[...]
+        results[number] = both[:, :COLS] + table_times(
+            (across_high, across_low), both[:, COLS:]
         )
-        copy = pltpu.make_async_copy(results.at[number], outs[number], out_sem.at[number])
+        copy = pltpu.make_async_copy(
+            results.at[number], sums_out.at[number], out_sem.at[number]
+        )
         copy.start()
         out_copies.append(copy)
 
+    mine = lax.broadcasted_iota(jnp.int32, (8, COLS), 0) == team
+    for number in range(OUTPUTS):
+        wait(part_in.at[number], 8, part_recv_sem.at[number], TEAMS)
+        total = sum(part_in[number, 8 * k : 8 * k + 8, :] for k in range(TEAMS))
+        carried[number] = jnp.where(mine, total, 0.0)
+    copy = pltpu.make_async_copy(carried, carry_out, out_sem.at[OUTPUTS])
+    copy.start()
+    out_copies.append(copy)
     for copy in out_copies:
         copy.wait()
     for number, group in enumerate(GROUPS):
         wait(sent, 4 * len(group), send_sem.at[number])
     for number in range(OUTPUTS):
-        wait(sent_back.at[number], 9, back_send_sem.at[number])
+        wait(sent_back.at[number], 8, back_send_sem.at[number])
+        wait(owed.at[number], 8, owed_send_sem.at[number], LANES)
+        wait(part_in.at[number], 8, part_send_sem.at[number], TEAMS)
+
+
+def carry_kernel(sums_in, carry_in, *refs):
+    outs = refs[:OUTPUTS]
+    sums, carry, results, load_sem, out_sem = refs[OUTPUTS:]
+    carry_copy = pltpu.make_async_copy(carry_in, carry, load_sem.at[OUTPUTS])
+    carry_copy.start()
+    copies = [
+        pltpu.make_async_copy(sums_in.at[k], sums.at[k], load_sem.at[k]) for k in range(OUTPUTS)
+    ]
+    for copy in copies:
+        copy.start()
+    shape = (2 * ROWS, COLS)
+    place = lax.broadcasted_iota(jnp.int32, shape, 0) * COLS + lax.broadcasted_iota(
+        jnp.int32, shape, 1
+    )
+    power = jnp.exp((place + 1).astype(jnp.float32) * (-1.0 / (2 * BLOCK)))
+    carry_copy.wait()
+    out_copies = []
+    for k in range(OUTPUTS):
+        copies[k].wait()
+        results[k] = sums[k] + jnp.sum(carry[k]) * power
+        copy = pltpu.make_async_copy(results.at[k], outs[k], out_sem.at[k])
+        copy.start()
+        out_copies.append(copy)
+    for copy in out_copies:
+        copy.wait()
 
 
 def local(*operands):
     limbs = [v.reshape(ROWS, COLS) for v in operands]
     constants = tables()
     anywhere = pl.BlockSpec(memory_space=pl.ANY)
-    sums = pl.pallas_call(
+    sums_shape = (OUTPUTS, 2 * ROWS, COLS)
+    sums, carry = pl.pallas_call(
         merge_kernel,
-        out_shape=[jax.ShapeDtypeStruct((2 * ROWS, COLS), jnp.float32)] * OUTPUTS,
+        out_shape=[
+            jax.ShapeDtypeStruct(sums_shape, jnp.float32),
+            jax.ShapeDtypeStruct((OUTPUTS, 8, COLS), jnp.float32),
+        ],
         in_specs=[anywhere] * (OPERANDS + len(constants)),
-        out_specs=[anywhere] * OUTPUTS,
+        out_specs=[anywhere] * 2,
         scratch_shapes=[
             *[pltpu.VMEM((ROWS, COLS), jnp.float32)] * OPERANDS,
             *[pltpu.VMEM(t.shape, t.dtype) for t in constants[:-1]],
@@ -379,20 +466,36 @@
             pltpu.VMEM((DEVICES * STEP_IN, COLS), jnp.float32),
             pltpu.VMEM((OUTPUTS, DEVICES * STEP_OUT, COLS), jnp.float32),
             pltpu.VMEM((OUTPUTS, DEVICES * STEP_OUT, COLS), jnp.float32),
-            pltpu.VMEM((OUTPUTS, 2 * ROWS, COLS), jnp.float32),
+            pltpu.VMEM(sums_shape, jnp.float32),
+            pltpu.VMEM((OUTPUTS, DEVICES, COLS), jnp.float32),
+            pltpu.VMEM((OUTPUTS, DEVICES, COLS), jnp.float32),
+            pltpu.VMEM((OUTPUTS, 8, COLS), jnp.float32),
+            pltpu.VMEM((OUTPUTS, 8 * TEAMS, COLS), jnp.float32),
+            pltpu.VMEM((OUTPUTS, 8, COLS), jnp.float32),
             pltpu.SemaphoreType.DMA((OPERANDS,)),
             pltpu.SemaphoreType.DMA((len(constants),)),
-            pltpu.SemaphoreType.DMA((OUTPUTS,)),
-            pltpu.SemaphoreType.DMA((len(GROUPS),)),
-            pltpu.SemaphoreType.DMA((len(GROUPS),)),
-            pltpu.SemaphoreType.DMA((OUTPUTS,)),
-            pltpu.SemaphoreType.DMA((OUTPUTS,)),
+            pltpu.SemaphoreType.DMA((OUTPUTS + 1,)),
+            *[pltpu.SemaphoreType.DMA((len(GROUPS),))] * 2,
+            *[pltpu.SemaphoreType.DMA((OUTPUTS,))] * 6,
         ],
         compiler_params=pltpu.CompilerParams(
             collective_id=0, has_side_effects=True, vmem_limit_bytes=56 << 20
         ),
     )(*limbs, *constants)
-    return tuple(s.reshape(-1) for s in sums)
+    results = pl.pallas_call(
+        carry_kernel,
+        out_shape=[jax.ShapeDtypeStruct(sums_shape[1:], jnp.float32)] * OUTPUTS,
+        in_specs=[anywhere] * 2,
+        out_specs=[anywhere] * OUTPUTS,
+        scratch_shapes=[
+            pltpu.VMEM(sums_shape, jnp.float32),
+            pltpu.VMEM((OUTPUTS, 8, COLS), jnp.float32),
+            pltpu.VMEM(sums_shape, jnp.float32),
+            pltpu.SemaphoreType.DMA((OUTPUTS + 1,)),
+            pltpu.SemaphoreType.DMA((OUTPUTS,)),
+        ],
+    )(sums, carry)
+    return tuple(r.reshape(-1) for r in results)
 
 
 def solution(mesh):

time: 69.1 us -> 57.8 us (0.84)
  the two profiles are of different devices: /device:TPU:3 before, /device:TPU:1 now
where the time goes in v2:
time: 57.8 us; the launch traced here: 56.7 us
  Pallas kernels  56 us (97%)
  between operations  0.64 us (1%)
    pallas_call x1, Pallas kernels, local(): pl.pallas_call(merge_kernel, out_shape=[jax.ShapeDtypeStruct(sums_shape,...  54 us
    pallas_call x1, Pallas kernels, local(): pl.pallas_call(carry_kernel, out_shape=[jax.ShapeDtypeStruct(sums_shape[1...  2.01 us

profile of v2, /device:TPU:1, one launch (start us, length us, event | category | flops | bytes accessed | tf_op | source)
XLA Modules:
  0.0 56.7 jit_solution(4373958444612867146)
XLA Ops:
  0.6 54.0 %shard_map.275 = (f32[2,512,128]{2,1,0:T(8,128)}, f32[2,8,128]{2,1,0:T(8,128)}) custom-call(f32[256,128]{1,0:T(8,128)} %bitcast.9, f32[256,128]{1,0:T(8,128)} %bitcast.10, f32[256,128]{1,0:T(8,128)} %bitcast.11, f32[256,128]{1,0:T(8,128)} %bitcast.12, f32[256,128]{1,0:T(8,128)} %bitcast.13, f32[256,128]{1,0:T(8,128)} %bitcast.14, f32[256,128]{1,0:T(8,128)} %bitcast.15, ...), custom_call_target="tpu_custom_call" | custom-call | tf_op jit(solution)/shard_map/pallas_call | solution.py:453
  54.7 2.0 %shard_map.276 = (f32[512,128]{1,0:T(8,128)}, f32[512,128]{1,0:T(8,128)}) custom-call(f32[2,512,128]{2,1,0:T(8,128)} %get-tuple-element.6.sums_in, f32[2,8,128]{2,1,0:T(8,128)} %get-tuple-element.7.carry_in), custom_call_target="tpu_custom_call" | custom-call | tf_op jit(solution)/shard_map/pallas_call | solution.py:485

commit v3 on v2

--- a/solution.py
+++ b/solution.py
@@ -33,6 +33,11 @@
 
 def as_real(table):
     return np.block([[table.real, -table.imag], [table.imag, table.real]])
+
+
+def by_half(table):
+    parts = table.reshape(2, 2, DEVICES, -1).transpose(1, 0, 2, 3)
+    return parts.reshape(4 * DEVICES, -1)
 
 
 def unit(turns):
@@ -62,8 +67,7 @@
     offset = col[None, :] - col[:, None]
     inside = np.where(offset >= 0, DECAY ** np.maximum(offset, 0), 0.0)
     ends = np.outer(DECAY ** (COLS - 1 - col), DECAY ** (col + 1))
-    line = np.arange(2 * ROWS, dtype=np.float64)
-    gap = line[:, None] - line[None, :] - 1
+    gap = row[:, None] - row[None, :] - 1
     across = np.where(gap >= 0, DECAY ** (COLS * np.maximum(gap, 0)), 0.0)
     phase = unit((np.arange(ROWS)[:, None] + ROWS * col[None, :] + 0.25) / BLOCK)
     ends_at = DECAY**BLOCK
@@ -88,7 +92,7 @@
     )
     middle = (
         *split(as_real(over_blocks)),
-        *split(as_real(back_blocks)),
+        *split(by_half(as_real(back_blocks))),
         *split(np.concatenate([carry.real, -carry.imag], axis=1)),
     )
     backward = (
@@ -115,9 +119,13 @@
     return dot(high, table[0][...]) + dot(high, table[1][...]) + dot(low, table[0][...])
 
 
+def table_times_halves(table, values):
+    high, low = values
+    return dot(table[0], high) + dot(table[1], high) + dot(table[0], low)
+
+
 def table_times(table, values):
-    high, low = halves(values)
-    return dot(table[0][...], high) + dot(table[1][...], high) + dot(table[0][...], low)
+    return table_times_halves((table[0][...], table[1][...]), halves(values))
 
 
 def complex_times(left, right):
@@ -143,15 +151,12 @@
         landed,
         sent_back,
         landed_back,
-        results,
         owed,
         owed_in,
         part,
         part_in,
-        carried,
         load_sem,
         table_sem,
-        out_sem,
         send_sem,
         recv_sem,
         back_send_sem,
@@ -208,22 +213,22 @@
         limb_copies[k].start()
     for k in range(6):
         table_copies[k].start()
+
+    def partner(i):
+        other = jnp.bitwise_xor(me, i)
+        return other, (lax.div(other, LANES), lax.rem(other, LANES))
+
+    barrier = pltpu.get_barrier_semaphore()
+
+    def greet(i, _):
+        pl.semaphore_signal(barrier, inc=1, device_id=partner(i)[1], device_id_type=MESH)
+        return 0
+
+    lax.fori_loop(1, DEVICES, greet, 0)
     for k in first_limbs[2:]:
         limb_copies[k].start()
     for k in range(6, count):
         table_copies[k].start()
-
-    def partner(i):
-        other = jnp.bitwise_xor(me, i)
-        return other, (lax.div(other, LANES), lax.rem(other, LANES))
-
-    barrier = pltpu.get_barrier_semaphore()
-
-    def greet(i, _):
-        pl.semaphore_signal(barrier, inc=1, device_id=partner(i)[1], device_id_type=MESH)
-        return 0
-
-    lax.fori_loop(1, DEVICES, greet, 0)
 
     def send(source, target, step, offset, size, send_to, recv_at):
         def go(i, _):
@@ -246,9 +251,8 @@
         whole = ref.at[pl.ds(0, (senders - 1) * size)]
         pltpu.make_async_copy(whole, whole, sem).wait()
 
-    need(0, 1, 2, 3, 4, 5)
-    for number, group in enumerate(GROUPS):
-        for place, k in enumerate(group):
+    def transform(number):
+        for place, k in enumerate(GROUPS[number]):
             limb_copies[k].wait()
             whole = limbs[k][...].astype(jnp.bfloat16)
             first = dot(rows_high[...], whole) + dot(rows_low[...], whole)
@@ -262,14 +266,15 @@
                     sent[pl.ds(start, DEVICES, stride=STEP_IN), :] = done[
                         s * DEVICES : (s + 1) * DEVICES, c * COLS : (c + 1) * COLS
                     ]
-        if number == 0:
-            pl.semaphore_wait(barrier, DEVICES - 1)
+
+    def send_group(number):
         send(
-            sent, landed, STEP_IN, 8 * number, 4 * len(group),
+            sent, landed, STEP_IN, 8 * number, 4 * len(GROUPS[number]),
             send_sem.at[number], recv_sem.at[number],
         )
 
     spectra = [None] * OPERANDS
+    multiplied = [None] * OUTPUTS
 
     def arrive(number):
         group = GROUPS[number]
@@ -288,7 +293,7 @@
     def tile(number):
         return pl.ds(pl.multiple_of(number * 8, 8), 8)
 
-    def give_back(number, terms):
+    def multiply(number, terms):
         terms = [complex_times(spectra[a], spectra[b]) for a, b in terms]
         product = (sum(t[0] for t in terms), sum(t[1] for t in terms))
         reached = [
@@ -317,18 +322,22 @@
 
         lax.fori_loop(1, LANES, owe, 0)
         owed_in[number, tile(lane), :] = owed[number, tile(lane), :]
-        back = table_times((back_high, back_low), jnp.concatenate(product, axis=0))
-        source = sent_back.at[number]
+        multiplied[number] = halves(jnp.concatenate(product, axis=0))
+
+    def invert(number, odd):
+        rows = slice(2 * odd * DEVICES, 2 * (odd + 1) * DEVICES)
+        back = table_times_halves((back_high[rows, :], back_low[rows, :]), multiplied[number])
+        source = sent_back.at[number, odd]
         for c in range(2):
-            for odd in range(2):
-                for s in range(2):
-                    start = (2 * c + odd) * DEVICES
-                    source[pl.ds((odd * 2 + s) * 2 + c, DEVICES, stride=STEP_OUT), :] = back[
-                        start : start + DEVICES, s * COLS : (s + 1) * COLS
-                    ]
+            for s in range(2):
+                source[pl.ds(2 * s + c, DEVICES, stride=STEP_OUT), :] = back[
+                    c * DEVICES : (c + 1) * DEVICES, s * COLS : (s + 1) * COLS
+                ]
+
+    def send_back(number, odd):
         send(
-            source, landed_back.at[number], STEP_OUT, 0, 8,
-            back_send_sem.at[number], back_recv_sem.at[number],
+            sent_back.at[number, odd], landed_back.at[number, odd], STEP_OUT, 0, 4,
+            back_send_sem.at[number, odd], back_recv_sem.at[number, odd],
         )
 
     def gather_owed(number):
@@ -349,99 +358,100 @@
         lax.fori_loop(1, TEAMS, pay, 0)
         part_in[number, tile(team), :] = part[number]
 
+    def finish(number, odd):
+        source = landed_back.at[number, odd]
+        wait(source, 4, back_recv_sem.at[number, odd])
+        spectrum = jnp.concatenate(
+            [
+                jnp.concatenate(
+                    [source[pl.ds(2 * s + c, DEVICES, stride=STEP_OUT), :] for c in range(2)],
+                    axis=1,
+                )
+                for s in range(2)
+            ],
+            axis=0,
+        )
+        first = times_table(spectrum, (cols_back_high, cols_back_low))
+        turned = complex_times(
+            (first[:, :COLS], first[:, COLS:]), (twist_real[...], -twist_imag[...])
+        )
+        coeffs = table_times((rows_back_high, rows_back_low), jnp.concatenate(turned, axis=0))
+        both = times_table(coeffs, (scan_high, scan_low))
+        sums_out[number, odd * ROWS : (odd + 1) * ROWS, :] = both[:, :COLS] + table_times(
+            (across_high, across_low), both[:, COLS:]
+        )
+
+    need(0, 1, 2, 3, 4, 5)
+    transform(0)
+    transform(1)
+    pl.semaphore_wait(barrier, DEVICES - 1)
+    send_group(0)
+    send_group(1)
+    transform(2)
+    transform(3)
+    send_group(2)
+    send_group(3)
     need(6, 7)
     arrive(0)
     arrive(1)
     need(8, 9, 10, 11, count - 1)
-    give_back(0, [(2, 1), (0, 3)])
+    multiply(0, [(2, 1), (0, 3)])
+    invert(0, 0)
+    send_back(0, 0)
+    invert(0, 1)
+    send_back(0, 1)
     arrive(2)
     arrive(3)
-    give_back(1, [(4, 1), (0, 5), (6, 3)])
-
+    multiply(1, [(4, 1), (0, 5), (6, 3)])
+    invert(1, 0)
+    send_back(1, 0)
+    invert(1, 1)
+    send_back(1, 1)
     gather_owed(0)
     gather_owed(1)
-
     need(*range(count))
-    out_copies = []
-    for number in range(OUTPUTS):
-        source = landed_back.at[number]
-        wait(source, 8, back_recv_sem.at[number])
-        coeffs = []
-        for odd in range(2):
-            spectrum = jnp.concatenate(
-                [
-                    jnp.concatenate(
-                        [
-                            source[
-                                pl.ds(4 * odd + 2 * s + c, DEVICES, stride=STEP_OUT), :
-                            ]
-                            for c in range(2)
-                        ],
-                        axis=1,
-                    )
-                    for s in range(2)
-                ],
-                axis=0,
-            )
-            first = times_table(spectrum, (cols_back_high, cols_back_low))
-            turned = complex_times(
-                (first[:, :COLS], first[:, COLS:]), (twist_real[...], -twist_imag[...])
-            )
-            coeffs.append(
-                table_times((rows_back_high, rows_back_low), jnp.concatenate(turned, axis=0))
-            )
-        both = times_table(jnp.concatenate(coeffs, axis=0), (scan_high, scan_low))
-        results[number] = both[:, :COLS] + table_times(
-            (across_high, across_low), both[:, COLS:]
-        )
-        copy = pltpu.make_async_copy(
-            results.at[number], sums_out.at[number], out_sem.at[number]
-        )
-        copy.start()
-        out_copies.append(copy)
+    finish(0, 0)
+    finish(0, 1)
+    finish(1, 0)
+    finish(1, 1)
 
     mine = lax.broadcasted_iota(jnp.int32, (8, COLS), 0) == team
     for number in range(OUTPUTS):
         wait(part_in.at[number], 8, part_recv_sem.at[number], TEAMS)
         total = sum(part_in[number, 8 * k : 8 * k + 8, :] for k in range(TEAMS))
-        carried[number] = jnp.where(mine, total, 0.0)
-    copy = pltpu.make_async_copy(carried, carry_out, out_sem.at[OUTPUTS])
-    copy.start()
-    out_copies.append(copy)
-    for copy in out_copies:
-        copy.wait()
+        carry_out[number] = jnp.where(mine, total, 0.0)
     for number, group in enumerate(GROUPS):
         wait(sent, 4 * len(group), send_sem.at[number])
     for number in range(OUTPUTS):
-        wait(sent_back.at[number], 8, back_send_sem.at[number])
+        for odd in range(2):
+            wait(sent_back.at[number, odd], 4, back_send_sem.at[number, odd])
         wait(owed.at[number], 8, owed_send_sem.at[number], LANES)
         wait(part_in.at[number], 8, part_send_sem.at[number], TEAMS)
 
 
-def carry_kernel(sums_in, carry_in, *refs):
+def carry_kernel(sums, carry, *refs):
     outs = refs[:OUTPUTS]
-    sums, carry, results, load_sem, out_sem = refs[OUTPUTS:]
-    carry_copy = pltpu.make_async_copy(carry_in, carry, load_sem.at[OUTPUTS])
-    carry_copy.start()
-    copies = [
-        pltpu.make_async_copy(sums_in.at[k], sums.at[k], load_sem.at[k]) for k in range(OUTPUTS)
-    ]
-    for copy in copies:
-        copy.start()
-    shape = (2 * ROWS, COLS)
+    results, out_sem = refs[OUTPUTS:]
+    shape = (ROWS, COLS)
     place = lax.broadcasted_iota(jnp.int32, shape, 0) * COLS + lax.broadcasted_iota(
         jnp.int32, shape, 1
     )
     power = jnp.exp((place + 1).astype(jnp.float32) * (-1.0 / (2 * BLOCK)))
-    carry_copy.wait()
-    out_copies = []
+    corner = place[:8, :] == 8 * COLS - 1
+    copies = []
     for k in range(OUTPUTS):
-        copies[k].wait()
-        results[k] = sums[k] + jnp.sum(carry[k]) * power
-        copy = pltpu.make_async_copy(results.at[k], outs[k], out_sem.at[k])
-        copy.start()
-        out_copies.append(copy)
-    for copy in out_copies:
+        incoming = jnp.sum(carry[k])
+        for odd in range(2):
+            rows = pl.ds(odd * ROWS, ROWS)
+            results[k, rows, :] = sums[k, rows, :] + incoming * power
+            copy = pltpu.make_async_copy(
+                results.at[k, rows], outs[k].at[rows], out_sem.at[k, odd]
+            )
+            copy.start()
+            copies.append(copy)
+            last = sums[k, (odd + 1) * ROWS - 8 : (odd + 1) * ROWS, :]
+            incoming = incoming * DECAY**BLOCK + jnp.sum(jnp.where(corner, last, 0.0))
+    for copy in copies:
         copy.wait()
 
 
@@ -449,6 +459,7 @@
     limbs = [v.reshape(ROWS, COLS) for v in operands]
     constants = tables()
     anywhere = pl.BlockSpec(memory_space=pl.ANY)
+    on_chip = pl.BlockSpec(memory_space=pltpu.VMEM)
     sums_shape = (OUTPUTS, 2 * ROWS, COLS)
     sums, carry = pl.pallas_call(
         merge_kernel,
@@ -457,43 +468,38 @@
             jax.ShapeDtypeStruct((OUTPUTS, 8, COLS), jnp.float32),
         ],
         in_specs=[anywhere] * (OPERANDS + len(constants)),
-        out_specs=[anywhere] * 2,
+        out_specs=[on_chip] * 2,
         scratch_shapes=[
             *[pltpu.VMEM((ROWS, COLS), jnp.float32)] * OPERANDS,
             *[pltpu.VMEM(t.shape, t.dtype) for t in constants[:-1]],
             pltpu.VMEM(constants[-1].shape[1:], jnp.float32),
             pltpu.VMEM((DEVICES * STEP_IN, COLS), jnp.float32),
             pltpu.VMEM((DEVICES * STEP_IN, COLS), jnp.float32),
-            pltpu.VMEM((OUTPUTS, DEVICES * STEP_OUT, COLS), jnp.float32),
-            pltpu.VMEM((OUTPUTS, DEVICES * STEP_OUT, COLS), jnp.float32),
-            pltpu.VMEM(sums_shape, jnp.float32),
+            *[pltpu.VMEM((OUTPUTS, 2, DEVICES * STEP_OUT, COLS), jnp.float32)] * 2,
             pltpu.VMEM((OUTPUTS, DEVICES, COLS), jnp.float32),
             pltpu.VMEM((OUTPUTS, DEVICES, COLS), jnp.float32),
             pltpu.VMEM((OUTPUTS, 8, COLS), jnp.float32),
             pltpu.VMEM((OUTPUTS, 8 * TEAMS, COLS), jnp.float32),
-            pltpu.VMEM((OUTPUTS, 8, COLS), jnp.float32),
             pltpu.SemaphoreType.DMA((OPERANDS,)),
             pltpu.SemaphoreType.DMA((len(constants),)),
-            pltpu.SemaphoreType.DMA((OUTPUTS + 1,)),
             *[pltpu.SemaphoreType.DMA((len(GROUPS),))] * 2,
-            *[pltpu.SemaphoreType.DMA((OUTPUTS,))] * 6,
+            *[pltpu.SemaphoreType.DMA((OUTPUTS, 2))] * 2,
+            *[pltpu.SemaphoreType.DMA((OUTPUTS,))] * 4,
         ],
         compiler_params=pltpu.CompilerParams(
-            collective_id=0, has_side_effects=True, vmem_limit_bytes=56 << 20
+            collective_id=0, has_side_effects=True, vmem_limit_bytes=40 << 20
         ),
-    )(*limbs, *constants)
+    )(*[pltpu.with_memory_space_constraint(v, pltpu.HBM) for v in (*limbs, *constants)])
     results = pl.pallas_call(
         carry_kernel,
         out_shape=[jax.ShapeDtypeStruct(sums_shape[1:], jnp.float32)] * OUTPUTS,
-        in_specs=[anywhere] * 2,
+        in_specs=[on_chip] * 2,
         out_specs=[anywhere] * OUTPUTS,
         scratch_shapes=[
             pltpu.VMEM(sums_shape, jnp.float32),
-            pltpu.VMEM((OUTPUTS, 8, COLS), jnp.float32),
-            pltpu.VMEM(sums_shape, jnp.float32),
-            pltpu.SemaphoreType.DMA((OUTPUTS + 1,)),
-            pltpu.SemaphoreType.DMA((OUTPUTS,)),
+            pltpu.SemaphoreType.DMA((OUTPUTS, 2)),
         ],
+        compiler_params=pltpu.CompilerParams(vmem_limit_bytes=8 << 20),
     )(sums, carry)
     return tuple(r.reshape(-1) for r in results)
 

time: 57.8 us -> 53.8 us (0.931); the launches traced: 56.7 us -> 53.3 us
  Pallas kernels: 56 us -> 52.7 us
    pallas_call x1, Pallas kernels: 54 us -> 51.8 us  [local(): pl.pallas_call(merge_kernel, out_shape=[jax.ShapeDtypeStruct(sums_shape,...]
    pallas_call x1, Pallas kernels: 2.01 us -> 0.95 us  [local(): pl.pallas_call(carry_kernel, out_shape=[jax.ShapeDtypeStruct(sums_shape[1...]
where the time goes in v3:
time: 53.8 us; the launch traced here: 53.3 us
  Pallas kernels  52.7 us (98%)
  between operations  0.64 us (1%)
    pallas_call x1, Pallas kernels, local(): pl.pallas_call(merge_kernel, out_shape=[jax.ShapeDtypeStruct(sums_shape,...  51.8 us

profile of v3, /device:TPU:1, one launch (start us, length us, event | category | flops | bytes accessed | tf_op | source)
XLA Modules:
  0.0 53.3 jit_solution(13418021985594328579)
XLA Ops:
  0.6 51.8 %shard_map.275 = (f32[2,512,128]{2,1,0:T(8,128)S(1)}, f32[2,8,128]{2,1,0:T(8,128)S(1)}) custom-call(f32[256,128]{1,0:T(8,128)} %bitcast.9, f32[256,128]{1,0:T(8,128)} %bitcast.10, f32[256,128]{1,0:T(8,128)} %bitcast.11, f32[256,128]{1,0:T(8,128)} %bitcast.12, f32[256,128]{1,0:T(8,128)} %bitcast.13, f32[256,128]{1,0:T(8,128)} %bitcast.14, ...), custom_call_target="tpu_custom_call" | custom-call | tf_op jit(solution)/shard_map/pallas_call | solution.py:464
  52.4 1.0 %shard_map.276 = (f32[512,128]{1,0:T(8,128)}, f32[512,128]{1,0:T(8,128)}) custom-call(f32[2,512,128]{2,1,0:T(8,128)S(1)} %get-tuple-element.6.sums, f32[2,8,128]{2,1,0:T(8,128)S(1)} %get-tuple-element.7.carry), custom_call_target="tpu_custom_call" | custom-call | tf_op jit(solution)/shard_map/pallas_call | solution.py:493

commit v4 on v3

--- a/solution.py
+++ b/solution.py
@@ -19,6 +19,7 @@
 DECAY = math.exp(-1.0 / (2 * BLOCK))
 LANES = 16
 TEAMS = 8
+RETURN = (8, 4)
 STEP_IN = 32
 STEP_OUT = 8
 GROUPS = ((0, 3), (2, 1), (4, 5), (6,))
@@ -165,6 +166,7 @@
         owed_recv_sem,
         part_send_sem,
         part_recv_sem,
+        relay_sem,
     ) = rest[OPERANDS + count - 1 :]
     (
         rows_high,
@@ -215,16 +217,28 @@
         table_copies[k].start()
 
     def partner(i):
-        other = jnp.bitwise_xor(me, i)
+        other = jnp.bitwise_xor(me, lax.rem(i * 37, DEVICES))
         return other, (lax.div(other, LANES), lax.rem(other, LANES))
 
     barrier = pltpu.get_barrier_semaphore()
 
-    def greet(i, _):
-        pl.semaphore_signal(barrier, inc=1, device_id=partner(i)[1], device_id_type=MESH)
+    def greet_lane(i, _):
+        other = jnp.bitwise_xor(lane, i)
+        pl.semaphore_signal(barrier, inc=1, device_id=(team, other), device_id_type=MESH)
         return 0
 
-    lax.fori_loop(1, DEVICES, greet, 0)
+    def greet_team(i, _):
+        other = jnp.bitwise_xor(team, i)
+        pl.semaphore_signal(barrier, inc=1, device_id=(other, lane), device_id_type=MESH)
+        return 0
+
+    def relay(i, _):
+        other = jnp.bitwise_xor(team, i)
+        pl.semaphore_signal(relay_sem, inc=1, device_id=(other, lane), device_id_type=MESH)
+        return 0
+
+    lax.fori_loop(1, LANES, greet_lane, 0)
+    lax.fori_loop(1, TEAMS, greet_team, 0)
     for k in first_limbs[2:]:
         limb_copies[k].start()
     for k in range(6, count):
@@ -327,16 +341,17 @@
     def invert(number, odd):
         rows = slice(2 * odd * DEVICES, 2 * (odd + 1) * DEVICES)
         back = table_times_halves((back_high[rows, :], back_low[rows, :]), multiplied[number])
-        source = sent_back.at[number, odd]
+        source = sent_back.at[number, number * odd]
+        shift = (1 - number) * 4 * odd
         for c in range(2):
             for s in range(2):
-                source[pl.ds(2 * s + c, DEVICES, stride=STEP_OUT), :] = back[
+                source[pl.ds(shift + 2 * s + c, DEVICES, stride=STEP_OUT), :] = back[
                     c * DEVICES : (c + 1) * DEVICES, s * COLS : (s + 1) * COLS
                 ]
 
     def send_back(number, odd):
         send(
-            sent_back.at[number, odd], landed_back.at[number, odd], STEP_OUT, 0, 4,
+            sent_back.at[number, odd], landed_back.at[number, odd], STEP_OUT, 0, RETURN[number],
             back_send_sem.at[number, odd], back_recv_sem.at[number, odd],
         )
 
@@ -359,12 +374,17 @@
         part_in[number, tile(team), :] = part[number]
 
     def finish(number, odd):
-        source = landed_back.at[number, odd]
-        wait(source, 4, back_recv_sem.at[number, odd])
+        source = landed_back.at[number, number * odd]
+        shift = (1 - number) * 4 * odd
+        if number or not odd:
+            wait(source, RETURN[number], back_recv_sem.at[number, odd])
         spectrum = jnp.concatenate(
             [
                 jnp.concatenate(
-                    [source[pl.ds(2 * s + c, DEVICES, stride=STEP_OUT), :] for c in range(2)],
+                    [
+                        source[pl.ds(shift + 2 * s + c, DEVICES, stride=STEP_OUT), :]
+                        for c in range(2)
+                    ],
                     axis=1,
                 )
                 for s in range(2)
@@ -383,8 +403,10 @@
 
     need(0, 1, 2, 3, 4, 5)
     transform(0)
+    pl.semaphore_wait(barrier, LANES + TEAMS - 2)
+    lax.fori_loop(1, TEAMS, relay, 0)
     transform(1)
-    pl.semaphore_wait(barrier, DEVICES - 1)
+    pl.semaphore_wait(relay_sem, TEAMS - 1)
     send_group(0)
     send_group(1)
     transform(2)
@@ -397,9 +419,8 @@
     need(8, 9, 10, 11, count - 1)
     multiply(0, [(2, 1), (0, 3)])
     invert(0, 0)
+    invert(0, 1)
     send_back(0, 0)
-    invert(0, 1)
-    send_back(0, 1)
     arrive(2)
     arrive(3)
     multiply(1, [(4, 1), (0, 5), (6, 3)])
@@ -423,8 +444,10 @@
     for number, group in enumerate(GROUPS):
         wait(sent, 4 * len(group), send_sem.at[number])
     for number in range(OUTPUTS):
-        for odd in range(2):
-            wait(sent_back.at[number, odd], 4, back_send_sem.at[number, odd])
+        for odd in range(1 + number):
+            wait(
+                sent_back.at[number, odd], RETURN[number], back_send_sem.at[number, odd]
+            )
         wait(owed.at[number], 8, owed_send_sem.at[number], LANES)
         wait(part_in.at[number], 8, part_send_sem.at[number], TEAMS)
 
@@ -485,6 +508,7 @@
             *[pltpu.SemaphoreType.DMA((len(GROUPS),))] * 2,
             *[pltpu.SemaphoreType.DMA((OUTPUTS, 2))] * 2,
             *[pltpu.SemaphoreType.DMA((OUTPUTS,))] * 4,
+            pltpu.SemaphoreType.REGULAR,
         ],
         compiler_params=pltpu.CompilerParams(
             collective_id=0, has_side_effects=True, vmem_limit_bytes=40 << 20

time: 53.8 us -> 52.4 us (0.974)
  Pallas kernels: 52.7 us -> 51.6 us
    pallas_call x1, Pallas kernels: 51.8 us -> 50.7 us  [local(): pl.pallas_call(merge_kernel, out_shape=[jax.ShapeDtypeStruct(sums_shape,...]
where the time goes in v4:
time: 52.4 us; the launch traced here: 52.3 us
  Pallas kernels  51.6 us (98%)
  between operations  0.64 us (1%)
    pallas_call x1, Pallas kernels, local(): pl.pallas_call(merge_kernel, out_shape=[jax.ShapeDtypeStruct(sums_shape,...  50.7 us

profile of v4, /device:TPU:1, one launch (start us, length us, event | category | flops | bytes accessed | tf_op | source)
XLA Modules:
  0.0 52.3 jit_solution(8187250907123469253)
XLA Ops:
  0.6 50.7 %shard_map.275 = (f32[2,512,128]{2,1,0:T(8,128)S(1)}, f32[2,8,128]{2,1,0:T(8,128)S(1)}) custom-call(f32[256,128]{1,0:T(8,128)} %bitcast.9, f32[256,128]{1,0:T(8,128)} %bitcast.10, f32[256,128]{1,0:T(8,128)} %bitcast.11, f32[256,128]{1,0:T(8,128)} %bitcast.12, f32[256,128]{1,0:T(8,128)} %bitcast.13, f32[256,128]{1,0:T(8,128)} %bitcast.14, ...), custom_call_target="tpu_custom_call" | custom-call | tf_op jit(solution)/shard_map/pallas_call | solution.py:487
  51.3 1.0 %shard_map.276 = (f32[512,128]{1,0:T(8,128)}, f32[512,128]{1,0:T(8,128)}) custom-call(f32[2,512,128]{2,1,0:T(8,128)S(1)} %get-tuple-element.6.sums, f32[2,8,128]{2,1,0:T(8,128)S(1)} %get-tuple-element.7.carry), custom_call_target="tpu_custom_call" | custom-call | tf_op jit(solution)/shard_map/pallas_call | solution.py:517

commit v5 on v4

--- a/solution.py
+++ b/solution.py
@@ -19,10 +19,10 @@
 DECAY = math.exp(-1.0 / (2 * BLOCK))
 LANES = 16
 TEAMS = 8
-RETURN = (8, 4)
 STEP_IN = 32
 STEP_OUT = 8
 GROUPS = ((0, 3), (2, 1), (4, 5), (6,))
+SIZES = (8, 8, 6, 6)
 MESH = pl.DeviceIdType.MESH
 
 
@@ -131,6 +131,12 @@
 
 def complex_times(left, right):
     return (left[0] * right[0] - left[1] * right[1], left[0] * right[1] + left[1] * right[0])
+
+
+def row_of(number, place, s, c):
+    if number < 2:
+        return 8 * s + 4 * number + 2 * place + c
+    return 16 + 8 * s + 4 * (number - 2) + 2 * place + c
 
 
 def block_of(ref, start):
@@ -266,50 +272,74 @@
         pltpu.make_async_copy(whole, whole, sem).wait()
 
     def transform(number):
-        for place, k in enumerate(GROUPS[number]):
+        for k in GROUPS[number]:
             limb_copies[k].wait()
-            whole = limbs[k][...].astype(jnp.bfloat16)
-            first = dot(rows_high[...], whole) + dot(rows_low[...], whole)
+        whole = jnp.concatenate([limbs[k][...] for k in GROUPS[number]], axis=1)
+        whole = whole.astype(jnp.bfloat16)
+        first = dot(rows_high[...], whole) + dot(rows_low[...], whole)
+        for place in range(len(GROUPS[number])):
+            cols = slice(place * COLS, (place + 1) * COLS)
             turned = complex_times(
-                (first[:ROWS], first[ROWS:]), (twist_real[...], twist_imag[...])
+                (first[:ROWS, cols], first[ROWS:, cols]), (twist_real[...], twist_imag[...])
             )
             done = times_table(jnp.concatenate(turned, axis=1), (cols_high, cols_low))
             for s in range(2):
                 for c in range(2):
-                    start = 8 * number + 4 * place + 2 * s + c
+                    start = row_of(number, place, s, c)
                     sent[pl.ds(start, DEVICES, stride=STEP_IN), :] = done[
                         s * DEVICES : (s + 1) * DEVICES, c * COLS : (c + 1) * COLS
                     ]
 
     def send_group(number):
         send(
-            sent, landed, STEP_IN, 8 * number, 4 * len(GROUPS[number]),
+            sent, landed, STEP_IN, 8 * number, SIZES[number],
             send_sem.at[number], recv_sem.at[number],
         )
 
-    spectra = [None] * OPERANDS
-    multiplied = [None] * OUTPUTS
-
-    def arrive(number):
-        group = GROUPS[number]
-        wait(landed, 4 * len(group), recv_sem.at[number])
-        for place, k in enumerate(group):
-            parts = [
-                jnp.concatenate(
-                    [block_of(landed, 8 * number + 4 * place + 2 * s + c) for s in range(2)],
-                    axis=1,
-                )
-                for c in range(2)
-            ]
-            both = table_times((over_high, over_low), jnp.concatenate(parts, axis=0))
-            spectra[k] = (both[: 2 * DEVICES], both[2 * DEVICES :])
+    by_s = [[] for _ in range(OPERANDS)]
+    bessel, harmonic = [], []
 
     def tile(number):
         return pl.ds(pl.multiple_of(number * 8, 8), 8)
 
-    def multiply(number, terms):
-        terms = [complex_times(spectra[a], spectra[b]) for a, b in terms]
-        product = (sum(t[0] for t in terms), sum(t[1] for t in terms))
+    def arrive_rest(s):
+        wait(landed, SIZES[2 + s], recv_sem.at[2 + s])
+        slots = [(number, place) for number in (2, 3) for place in range(len(GROUPS[number]))]
+        parts = [
+            jnp.concatenate(
+                [block_of(landed, row_of(number, place, s, c)) for number, place in slots], axis=1
+            )
+            for c in range(2)
+        ]
+        both = table_times((over_high, over_low), jnp.concatenate(parts, axis=0))
+        for slot, (number, place) in enumerate(slots):
+            cols = slice(slot * COLS, (slot + 1) * COLS)
+            by_s[GROUPS[number][place]].append(
+                (both[: 2 * DEVICES, cols], both[2 * DEVICES :, cols])
+            )
+        terms = [complex_times(by_s[a][s], by_s[b][s]) for a, b in ((4, 1), (0, 5), (6, 3))]
+        harmonic.append((sum(t[0] for t in terms), sum(t[1] for t in terms)))
+
+    def invert_half(number, s):
+        piece = (bessel, harmonic)[number][s]
+        product = halves(jnp.concatenate(piece, axis=0))
+        back = table_times_halves((back_high[...], back_low[...]), product)
+        for part in range(4):
+            sent_back[number, s, pl.ds(part, DEVICES, stride=STEP_OUT), :] = back[
+                part * DEVICES : (part + 1) * DEVICES
+            ]
+
+    def send_back(number, s):
+        send(
+            sent_back.at[number, s], landed_back.at[number, s], STEP_OUT, 0, 4,
+            back_send_sem.at[number, s], back_recv_sem.at[number, s],
+        )
+
+    def settle(number):
+        pieces = (bessel, harmonic)[number]
+        product = tuple(
+            jnp.concatenate([piece[c] for piece in pieces], axis=1) for c in range(2)
+        )
         reached = [
             complex_times(
                 (product[0][:, s * COLS : (s + 1) * COLS], product[1][:, s * COLS : (s + 1) * COLS]),
@@ -336,24 +366,22 @@
 
         lax.fori_loop(1, LANES, owe, 0)
         owed_in[number, tile(lane), :] = owed[number, tile(lane), :]
-        multiplied[number] = halves(jnp.concatenate(product, axis=0))
-
-    def invert(number, odd):
-        rows = slice(2 * odd * DEVICES, 2 * (odd + 1) * DEVICES)
-        back = table_times_halves((back_high[rows, :], back_low[rows, :]), multiplied[number])
-        source = sent_back.at[number, number * odd]
-        shift = (1 - number) * 4 * odd
-        for c in range(2):
-            for s in range(2):
-                source[pl.ds(shift + 2 * s + c, DEVICES, stride=STEP_OUT), :] = back[
-                    c * DEVICES : (c + 1) * DEVICES, s * COLS : (s + 1) * COLS
-                ]
-
-    def send_back(number, odd):
-        send(
-            sent_back.at[number, odd], landed_back.at[number, odd], STEP_OUT, 0, RETURN[number],
-            back_send_sem.at[number, odd], back_recv_sem.at[number, odd],
-        )
+
+    def arrive_half(s):
+        wait(landed, SIZES[s], recv_sem.at[s])
+        for number in range(2):
+            parts = [
+                jnp.concatenate(
+                    [block_of(landed, row_of(number, place, s, c)) for place in range(2)], axis=1
+                )
+                for c in range(2)
+            ]
+            both = table_times((over_high, over_low), jnp.concatenate(parts, axis=0))
+            for place, k in enumerate(GROUPS[number]):
+                cols = slice(place * COLS, (place + 1) * COLS)
+                by_s[k].append((both[: 2 * DEVICES, cols], both[2 * DEVICES :, cols]))
+        terms = [complex_times(by_s[a][s], by_s[b][s]) for a, b in ((2, 1), (0, 3))]
+        bessel.append((terms[0][0] + terms[1][0], terms[0][1] + terms[1][1]))
 
     def gather_owed(number):
         wait(owed_in.at[number], 8, owed_recv_sem.at[number], LANES)
@@ -374,22 +402,16 @@
         part_in[number, tile(team), :] = part[number]
 
     def finish(number, odd):
-        source = landed_back.at[number, number * odd]
-        shift = (1 - number) * 4 * odd
-        if number or not odd:
-            wait(source, RETURN[number], back_recv_sem.at[number, odd])
+        if not odd:
+            for s in range(2):
+                wait(landed_back.at[number, s], 4, back_recv_sem.at[number, s])
+
+        def piece(s, c):
+            row = pl.ds(2 * odd + c, DEVICES, stride=STEP_OUT)
+            return landed_back[number, s, row, :]
+
         spectrum = jnp.concatenate(
-            [
-                jnp.concatenate(
-                    [
-                        source[pl.ds(shift + 2 * s + c, DEVICES, stride=STEP_OUT), :]
-                        for c in range(2)
-                    ],
-                    axis=1,
-                )
-                for s in range(2)
-            ],
-            axis=0,
+            [jnp.concatenate([piece(s, c) for c in range(2)], axis=1) for s in range(2)], axis=0
         )
         first = times_table(spectrum, (cols_back_high, cols_back_low))
         turned = complex_times(
@@ -414,24 +436,25 @@
     send_group(2)
     send_group(3)
     need(6, 7)
-    arrive(0)
-    arrive(1)
+    arrive_half(0)
     need(8, 9, 10, 11, count - 1)
-    multiply(0, [(2, 1), (0, 3)])
-    invert(0, 0)
-    invert(0, 1)
+    invert_half(0, 0)
     send_back(0, 0)
-    arrive(2)
-    arrive(3)
-    multiply(1, [(4, 1), (0, 5), (6, 3)])
-    invert(1, 0)
+    arrive_half(1)
+    invert_half(0, 1)
+    send_back(0, 1)
+    arrive_rest(0)
+    invert_half(1, 0)
     send_back(1, 0)
-    invert(1, 1)
+    arrive_rest(1)
+    settle(0)
+    settle(1)
+    invert_half(1, 1)
     send_back(1, 1)
     gather_owed(0)
-    gather_owed(1)
     need(*range(count))
     finish(0, 0)
+    gather_owed(1)
     finish(0, 1)
     finish(1, 0)
     finish(1, 1)
@@ -441,13 +464,11 @@
         wait(part_in.at[number], 8, part_recv_sem.at[number], TEAMS)
         total = sum(part_in[number, 8 * k : 8 * k + 8, :] for k in range(TEAMS))
         carry_out[number] = jnp.where(mine, total, 0.0)
-    for number, group in enumerate(GROUPS):
-        wait(sent, 4 * len(group), send_sem.at[number])
+    for number, size in enumerate(SIZES):
+        wait(sent, size, send_sem.at[number])
     for number in range(OUTPUTS):
-        for odd in range(1 + number):
-            wait(
-                sent_back.at[number, odd], RETURN[number], back_send_sem.at[number, odd]
-            )
+        for odd in range(2):
+            wait(sent_back.at[number, odd], 4, back_send_sem.at[number, odd])
         wait(owed.at[number], 8, owed_send_sem.at[number], LANES)
         wait(part_in.at[number], 8, part_send_sem.at[number], TEAMS)
 

time: 52.4 us -> 51.6 us (0.985)
  Pallas kernels: 51.6 us -> 50.8 us
    pallas_call x1, Pallas kernels: 50.7 us -> 49.8 us  [local(): pl.pallas_call(merge_kernel, out_shape=[jax.ShapeDtypeStruct(sums_shape,...]
where the time goes in v5:
time: 51.6 us; the launch traced here: 51.4 us
  Pallas kernels  50.8 us (98%)
  between operations  0.64 us (1%)
    pallas_call x1, Pallas kernels, local(): pl.pallas_call(merge_kernel, out_shape=[jax.ShapeDtypeStruct(sums_shape,...  49.8 us

profile of v5, /device:TPU:1, one launch (start us, length us, event | category | flops | bytes accessed | tf_op | source)
XLA Modules:
  0.0 51.4 jit_solution(16837016045030031675)
XLA Ops:
  0.6 49.8 %shard_map.275 = (f32[2,512,128]{2,1,0:T(8,128)S(1)}, f32[2,8,128]{2,1,0:T(8,128)S(1)}) custom-call(f32[256,128]{1,0:T(8,128)} %bitcast.9, f32[256,128]{1,0:T(8,128)} %bitcast.10, f32[256,128]{1,0:T(8,128)} %bitcast.11, f32[256,128]{1,0:T(8,128)} %bitcast.12, f32[256,128]{1,0:T(8,128)} %bitcast.13, f32[256,128]{1,0:T(8,128)} %bitcast.14, ...), custom_call_target="tpu_custom_call" | custom-call | tf_op jit(solution)/shard_map/pallas_call | solution.py:508
  50.5 1.0 %shard_map.276 = (f32[512,128]{1,0:T(8,128)}, f32[512,128]{1,0:T(8,128)}) custom-call(f32[2,512,128]{2,1,0:T(8,128)S(1)} %get-tuple-element.6.sums, f32[2,8,128]{2,1,0:T(8,128)S(1)} %get-tuple-element.7.carry), custom_call_target="tpu_custom_call" | custom-call | tf_op jit(solution)/shard_map/pallas_call | solution.py:538

commit v6 on v5

--- a/solution.py
+++ b/solution.py
@@ -446,8 +446,8 @@
     arrive_rest(0)
     invert_half(1, 0)
     send_back(1, 0)
+    settle(0)
     arrive_rest(1)
-    settle(0)
     settle(1)
     invert_half(1, 1)
     send_back(1, 1)

time: 51.6 us -> 51.5 us (level)
  no operation moved by 1% of the time
where the time goes in v6:
time: 51.5 us; the launch traced here: 51.4 us
  Pallas kernels  50.8 us (99%)
  between operations  0.64 us (1%)
    pallas_call x1, Pallas kernels, local(): pl.pallas_call(merge_kernel, out_shape=[jax.ShapeDtypeStruct(sums_shape,...  49.8 us

profile of v6, /device:TPU:1, one launch (start us, length us, event | category | flops | bytes accessed | tf_op | source)
XLA Modules:
  0.0 51.4 jit_solution(11786532258598589563)
XLA Ops:
  0.6 49.8 %shard_map.275 = (f32[2,512,128]{2,1,0:T(8,128)S(1)}, f32[2,8,128]{2,1,0:T(8,128)S(1)}) custom-call(f32[256,128]{1,0:T(8,128)} %bitcast.9, f32[256,128]{1,0:T(8,128)} %bitcast.10, f32[256,128]{1,0:T(8,128)} %bitcast.11, f32[256,128]{1,0:T(8,128)} %bitcast.12, f32[256,128]{1,0:T(8,128)} %bitcast.13, f32[256,128]{1,0:T(8,128)} %bitcast.14, ...), custom_call_target="tpu_custom_call" | custom-call | tf_op jit(solution)/shard_map/pallas_call | solution.py:508
  50.4 1.0 %shard_map.276 = (f32[512,128]{1,0:T(8,128)}, f32[512,128]{1,0:T(8,128)}) custom-call(f32[2,512,128]{2,1,0:T(8,128)S(1)} %get-tuple-element.6.sums, f32[2,8,128]{2,1,0:T(8,128)S(1)} %get-tuple-element.7.carry), custom_call_target="tpu_custom_call" | custom-call | tf_op jit(solution)/shard_map/pallas_call | solution.py:538
